TPU v7x, 32 devices: a whole 2x2x4 slice. The times are simulated.
32 devices in a mesh: pair: 8 (over y, x, core), row: 4 (over z).
Axes of the slice: x: 2, y: 2, z: 4, core: 2. Of those that a mesh axis runs over, the one named last changes fastest.
Arguments:
- amplitudes: bfloat16 [3, 160, 32, 5120], P(None, 'pair', 'row'), may hold values from -6 to 6
- integrals: bfloat16 [3, 5120, 5120], P(None, 'row', 'pair'), may hold values from -0.078125 to 0.078125
- occupied_irrep: int32 [32], replicated, may hold values from 0 to 7
- virtual_order: int32 [1280], replicated, may hold values from 0 to 1279, each once
- block_irreps: int32 [3], replicated, may hold values from 0 to 7
- occupied_energy: float32 [32], replicated, may hold values from -2 to -0.5
- virtual_energy: float32 [1280], replicated, may hold values from 1 to 4
Outputs:
- update: float32 [3, 160, 32, 5120], P(None, None, 'row', 'pair')
Inputs may be any that keep to these rules, and one draw needn't show every extreme that they name: virtual_order holds every virtual orbital once; entries g * 160 to g * 160 + 159 are the virtual orbitals of irrep g.
All inputs are finite; a program needn't handle non-finite values.
Results may differ from a plain program's by a relative error of at most 0.0003.
Values may be sent and summed in bfloat16 or wider, within the bound.
A program may use at most 128 MiB of HBM per device.

v0:
```python
import jax
import jax.numpy as jnp
from jax import lax
from jax.sharding import PartitionSpec as P

VIRG = 160


def shift_table(occupied_irrep, virtual_order, block_irreps, occupied_energy, virtual_energy):
    count_virt = virtual_energy.shape[0]
    orbital_ids = jnp.arange(count_virt, dtype=jnp.int32)
    matches = virtual_order[:, None] == orbital_ids[None, :]
    slot_energy = jnp.sum(jnp.where(matches, virtual_energy[None, :], jnp.float32(0.0)), axis=1)
    irrep_count = count_virt // VIRG
    energy_grid = slot_energy.reshape(irrep_count, VIRG)
    pair_irrep = jnp.bitwise_xor(block_irreps[:, None], occupied_irrep[None, :])
    irrep_ids = jnp.arange(irrep_count, dtype=jnp.int32)
    chosen = pair_irrep[:, None, None, :] == irrep_ids[None, :, None, None]
    picked = jnp.sum(jnp.where(chosen, energy_grid[None, :, :, None], jnp.float32(0.0)), axis=1)
    return picked - occupied_energy[None, None, :]


def body(
    amplitudes,
    integrals,
    occupied_irrep,
    virtual_order,
    block_irreps,
    occupied_energy,
    virtual_energy,
):
    block_count, virt_local, occ_local, pair_width = amplitudes.shape
    column_width = integrals.shape[2]
    shift = shift_table(
        occupied_irrep, virtual_order, block_irreps, occupied_energy, virtual_energy
    )
    occ_start = lax.axis_index("row") * occ_local
    col_start = lax.axis_index("pair") * column_width
    results = []
    for block in range(block_count):
        whole_rows = lax.all_gather(integrals[block], "row", axis=0, tiled=True)
        piece = lax.all_gather(amplitudes[block], "pair", axis=0, tiled=True)
        flat = piece.reshape(piece.shape[0] * piece.shape[1], piece.shape[2])
        product = jnp.dot(flat, whole_rows, preferred_element_type=jnp.float32)
        cycle_term = product.reshape(piece.shape[0], piece.shape[1], whole_rows.shape[1])
        row_shift = lax.dynamic_slice_in_dim(shift[block], occ_start, occ_local, 1)
        col_shift = lax.dynamic_slice_in_dim(
            shift[block].reshape(pair_width), col_start, column_width, 0
        )
        denominator = row_shift[:, :, None] + col_shift[None, None, :]
        results.append(cycle_term / denominator)
    return jnp.stack(results)


def solution(mesh):
    placed = (P(None, "pair", "row", None), P(None, "row", "pair"), P(), P(), P(), P(), P())
    return jax.shard_map(
        body, mesh=mesh, in_specs=placed, out_specs=P(None, None, "row", "pair"), check_vma=False
    )
```

profile of v0, /device:TPU:0, one launch (start us, length us, event | category | flops | bytes accessed | tf_op | source)
XLA Modules:
  0.0 626.3 jit_solution(1180767231952461776)
XLA Ops:
  6.5 0.0 all-gather.19.cloned.1.call-start
  6.5 4.8 fusion.21
  11.4 0.0 all-gather.19.cloned.1.call-update
  11.4 0.0 all-gather.17.cloned.1.call-start
  11.5 4.7 slice_bitcast_fusion.2
  16.2 0.0 copy-start.3
  16.2 0.0 all-gather.17.cloned.1.call-update
  16.2 0.0 all-gather.15.cloned.1.call-start
  16.3 0.7 all-gather.15.cloned.1.call-update
  17.0 0.0 all-gather.13.cloned.1.call-start
  17.0 0.5 all-gather.13.cloned.1.call-update
  17.5 0.0 all-gather.23.cloned.1.call-start
  17.6 0.5 all-gather.23.cloned.1.call-update
  18.1 0.0 all-gather.21.cloned.1.call-start
  18.2 0.5 all-gather.21.cloned.1.call-update
  18.7 0.0 copy-done.1
  18.7 0.0 copy-done.2
  18.7 1.0 select_reduce_fusion
  19.7 0.1 broadcast_in_dim.51
  19.8 0.0 copy-done.4
  19.8 0.0 copy-done.5
  19.8 0.1 broadcast_xor_fusion
  19.9 0.2 select_reduce_fusion.1
  20.0 0.0 copy-done.3
  20.0 0.1 broadcast_subtract_fusion
  20.1 0.1 copy.22
  20.2 0.1 reshape_squeeze.10
  20.3 0.1 copy.21
  20.4 0.1 copy.19
  20.6 0.1 reshape_squeeze.9
  20.6 0.1 dynamic_slice.21
  20.7 0.1 dynamic_slice.19
  20.8 0.1 copy.18
  20.9 0.1 copy.25
  21.0 0.1 reshape_squeeze.11
  21.1 0.1 dynamic_slice.23
  21.2 0.1 copy.24
  21.3 112.6 %all-gather.19.cloned.1.call-done = bf16[1,5120,640]{2,1,0:T(8,128)(2,1)} async-done(((bf16[1,1280,640]{2,1,0:T(8,128)(2,1)}), bf16[1,5120,640]{2,1,0:T(8,128)(2,1)}) %all-gather.19.cloned.1.call-update) | async-done | bytes 6553616 | tf_op jit(solution)/shard_map/all_gather | solution.py:41
  133.9 74.5 %all-gather.17.cloned.1.call-done = bf16[1,160,8,5120]{3,2,0,1:T(8,128)(2,1)} async-done(((bf16[1,20,8,5120]{3,2,0,1:T(8,128)(2,1)}), bf16[1,160,8,5120]{3,2,0,1:T(8,128)(2,1)}) %all-gather.17.cloned.1.call-update) | async-done | bytes 13107216 | tf_op jit(solution)/shard_map/all_gather | solution.py:42
  208.4 15.1 %divide_bitcast_fusion.1 = f32[1,160,8,640]{3,2,1,0:T(8,128)S(1)} fusion(bf16[1,5120,640]{2,1,0:T(8,128)(2,1)} %all-gather.19.cloned.1.call-done, bf16[1,160,8,5120]{3,2,0,1:T(8,128)(2,1)} %all-gather.17.cloned.1.call-done, f32[640]{0:T(1024)S(1)} %dynamic_slice.21, f32[160,8]{1,0:T(8,128)S(1)} %copy.21), kind=kOutput, calls=%fused_computation.13 | convolution fusion | flops 8390246400 | bytes 22945280 | tf_op jit(solution)/shard_map/dot_general | solution.py:44
  223.6 106.1 %all-gather.15.cloned.1.call-done = bf16[1,5120,640]{2,1,0:T(8,128)(2,1)} async-done(((bf16[1,1280,640]{2,1,0:T(8,128)(2,1)}), bf16[1,5120,640]{2,1,0:T(8,128)(2,1)}) %all-gather.15.cloned.1.call-update) | async-done | bytes 6553616 | tf_op jit(solution)/shard_map/all_gather | solution.py:41
  329.7 74.4 %all-gather.13.cloned.1.call-done = bf16[1,160,8,5120]{3,2,0,1:T(8,128)(2,1)} async-done(((bf16[1,20,8,5120]{3,2,0,1:T(8,128)(2,1)}), bf16[1,160,8,5120]{3,2,0,1:T(8,128)(2,1)}) %all-gather.13.cloned.1.call-update) | async-done | bytes 13107216 | tf_op jit(solution)/shard_map/all_gather | solution.py:42
  404.0 16.0 %divide_bitcast_fusion.2 = f32[1,160,8,640]{3,2,1,0:T(8,128)} fusion(bf16[1,5120,640]{2,1,0:T(8,128)(2,1)} %all-gather.15.cloned.1.call-done, bf16[1,160,8,5120]{3,2,0,1:T(8,128)(2,1)} %all-gather.13.cloned.1.call-done, f32[640]{0:T(1024)S(1)} %dynamic_slice.19, f32[160,8]{1,0:T(8,128)S(1)} %copy.18), kind=kOutput, calls=%fused_computation.14 | convolution fusion | flops 8390246400 | bytes 22945280 | tf_op jit(solution)/shard_map/dot_general | solution.py:44
  420.0 105.1 %all-gather.23.cloned.1.call-done = bf16[1,5120,640]{2,1,0:T(8,128)(2,1)} async-done(((bf16[1,1280,640]{2,1,0:T(8,128)(2,1)}), bf16[1,5120,640]{2,1,0:T(8,128)(2,1)}) %all-gather.23.cloned.1.call-update) | async-done | bytes 6553616 | tf_op jit(solution)/shard_map/all_gather | solution.py:41
  525.1 74.4 %all-gather.21.cloned.1.call-done = bf16[1,160,8,5120]{3,2,0,1:T(8,128)(2,1)} async-done(((bf16[1,20,8,5120]{3,2,0,1:T(8,128)(2,1)}), bf16[1,160,8,5120]{3,2,0,1:T(8,128)(2,1)}) %all-gather.21.cloned.1.call-update) | async-done | bytes 13107216 | tf_op jit(solution)/shard_map/all_gather | solution.py:42
  599.5 15.3 %divide_bitcast_fusion = f32[1,160,8,640]{3,2,1,0:T(8,128)S(1)} fusion(bf16[1,5120,640]{2,1,0:T(8,128)(2,1)} %all-gather.23.cloned.1.call-done, bf16[1,160,8,5120]{3,2,0,1:T(8,128)(2,1)} %all-gather.21.cloned.1.call-done, f32[640]{0:T(1024)S(1)} %dynamic_slice.23, f32[160,8]{1,0:T(8,128)S(1)} %copy.24), kind=kOutput, calls=%fused_computation.12 | convolution fusion | flops 8390246400 | bytes 22945280 | tf_op jit(solution)/shard_map/dot_general | solution.py:44
  614.8 0.0 copy-done
  614.8 4.7 pad_maximum_fusion
  (10 shorter events, 0.0 us)
Async XLA Ops:
  6.5 127.4 %all-gather.19.cloned.1.call-start = ((), (), s32[]{:S(2)}) async-start(), calls=%async_computation.3 | async-start | bytes 8192000 | tf_op jit(solution)/shard_map/all_gather | solution.py:41
  11.4 197.0 %all-gather.17.cloned.1.call-start = ((), (), s32[]{:S(2)}) async-start(), calls=%async_computation.2 | async-start | bytes 14745600 | tf_op jit(solution)/shard_map/all_gather | solution.py:42
  16.2 2.5 copy-start.1
  16.2 2.5 copy-start.2
  16.2 3.6 copy-start.4
  16.2 3.6 copy-start.5
  16.2 3.9 copy-start.3
  16.2 313.4 %all-gather.15.cloned.1.call-start = ((), (), s32[]{:S(2)}) async-start(), calls=%async_computation.1 | async-start | bytes 8192000 | tf_op jit(solution)/shard_map/all_gather | solution.py:41
  17.0 387.1 %all-gather.13.cloned.1.call-start = ((), (), s32[]{:S(2)}) async-start(), calls=%async_computation | async-start | bytes 14745600 | tf_op jit(solution)/shard_map/all_gather | solution.py:42
  17.5 507.6 %all-gather.23.cloned.1.call-start = ((), (), s32[]{:S(2)}) async-start(), calls=%async_computation.5 | async-start | bytes 8192000 | tf_op jit(solution)/shard_map/all_gather | solution.py:41
  18.1 581.3 %all-gather.21.cloned.1.call-start = ((), (), s32[]{:S(2)}) async-start(), calls=%async_computation.4 | async-start | bytes 14745600 | tf_op jit(solution)/shard_map/all_gather | solution.py:42
  599.5 15.3 %copy-start = (f32[1,160,8,640]{3,2,1,0:T(8,128)S(1)}, f32[1,160,8,640]{3,2,1,0:T(8,128)}, u32[]{:S(2)}) copy-start(f32[1,160,8,640]{3,2,1,0:T(8,128)} %divide_bitcast_fusion.2) | copy-start | bytes 9830404
Sparse Core Ops, SparseCore 0:
  11.5 122.3 all-gather.18
  135.8 72.5 all-gather.16
  210.0 119.6 all-gather.14
  331.4 72.5 all-gather.12
  405.4 119.6 all-gather.22
  526.9 72.5 all-gather.20
where the time goes:
time: 626 us
  waiting for transfers between devices  549 us (88%)
  matrix products  46.4 us (7%)
  between operations  13.6 us (2%)
  local copies, waits for them, and re-layouts  10.8 us (2%)
    all_gather x3, waiting for transfers between devices, body(): whole_rows = lax.all_gather(integrals[block], 'row', axis=0, tiled=True)  324 us
    all_gather x3, waiting for transfers between devices, body(): piece = lax.all_gather(amplitudes[block], 'pair', axis=0, tiled=True)  223 us
    dot_general x3, matrix products, body(): product = jnp.dot(flat, whole_rows, preferred_element_type=jnp.float32)  46.4 us
  transfers between devices with their start and end apart: 6, of which 6 were waited for; matrix products, arithmetic and copies ran while one was open for 6% of the time, Pallas kernels for 0%

commit v1 on v0

--- a/solution.py
+++ b/solution.py
@@ -38,7 +38,18 @@
     col_start = lax.axis_index("pair") * column_width
     results = []
     for block in range(block_count):
-        whole_rows = lax.all_gather(integrals[block], "row", axis=0, tiled=True)
+        ways = lax.axis_size("row")
+        up = [(d, (d + 1) % ways) for d in range(ways)]
+        down = [(d, (d - 1) % ways) for d in range(ways)]
+        earlier, later = ([integrals[block]], [integrals[block]])
+        for _ in range(ways // 2):
+            earlier.append(lax.ppermute(earlier[-1], "row", up))
+        for _ in range((ways - 1) // 2):
+            later.append(lax.ppermute(later[-1], "row", down))
+        line = jnp.concatenate([*earlier[::-1], *later[1:]], axis=0)
+        whole_rows = jnp.roll(
+            line, (lax.axis_index("row") - ways // 2) * integrals[block].shape[0], axis=0
+        )
         piece = lax.all_gather(amplitudes[block], "pair", axis=0, tiled=True)
         flat = piece.reshape(piece.shape[0] * piece.shape[1], piece.shape[2])
         product = jnp.dot(flat, whole_rows, preferred_element_type=jnp.float32)

time: 626 us -> 441 us (0.70)
  the two profiles are of different devices: /device:TPU:0 before, /device:TPU:24 now
where the time goes in v1:
time: 441 us; the launch traced here: 440 us
  waiting for transfers between devices  237 us (54%)
  matrix products  146 us (33%)
  local copies, waits for them, and re-layouts  25 us (6%)
  between operations  13.3 us (3%)
  starting transfers between devices  11.8 us (3%)
  other arithmetic  7.29 us (2%)
    ppermute x6, waiting for transfers between devices, body(): earlier.append(lax.ppermute(earlier[-1], 'row', up))  235 us
    dot_general x3, matrix products, body(): product = jnp.dot(flat, whole_rows, preferred_element_type=jnp.float32)  146 us
    dot_general x3, local copies, waits for them, and re-layouts, body(): product = jnp.dot(flat, whole_rows, preferred_element_type=jnp.float32)  12.6 us
  transfers between devices with their start and end apart: 12, of which 4 were waited for; matrix products, arithmetic and copies ran while one was open for 27% of the time, Pallas kernels for 0%

profile of v1, /device:TPU:24, one launch (start us, length us, event | category | flops | bytes accessed | tf_op | source)
XLA Modules:
  0.0 440.4 jit_solution(6312621475817813314)
XLA Ops:
  6.5 4.8 %slice_bitcast_fusion.4 = (bf16[1,20,8,5120]{3,2,0,1:T(8,128)(2,1)}, bf16[1,20,8,5120]{3,2,0,1:T(8,128)(2,1)}, bf16[1,20,8,5120]{3,2,0,1:T(8,128)(2,1)}) fusion(bf16[3,20,8,5120]{3,2,1,0:T(8,128)(2,1)} %param.9), kind=kLoop, calls=%fused_computation.64 | loop fusion | bytes 9830400
  11.3 0.0 all-gather.7.cloned.1.call-update
  11.3 0.0 all-gather.9.cloned.1.call-start
  11.4 0.6 all-gather.9.cloned.1.call-update
  12.1 0.0 all-gather.11.cloned.1.call-start
  12.1 0.7 all-gather.11.cloned.1.call-update
  12.8 4.5 %slice_bitcast_fusion.5 = (bf16[1280,640]{1,0:T(8,128)(2,1)S(1)}, bf16[1280,640]{1,0:T(8,128)(2,1)}, bf16[1280,640]{1,0:T(8,128)(2,1)}) fusion(bf16[3,1280,640]{2,1,0:T(8,128)(2,1)} %param.10), kind=kLoop, calls=%fused_computation.65 | loop fusion | bytes 9830400 | tf_op jit(solution)/shard_map/squeeze | solution.py:44
  17.4 2.0 collective-permute-start.2
  19.4 1.8 collective-permute-start.3
  21.2 0.2 collective-permute-start.5
  21.4 3.6 collective-permute-start.6
  25.0 66.2 %collective-permute-done = bf16[1280,640]{1,0:T(8,128)(2,1)} collective-permute-done((bf16[1280,640]{1,0:T(8,128)(2,1)S(1)}, bf16[1280,640]{1,0:T(8,128)(2,1)}, u32[]{:S(2)}, u32[]{:S(2)}) %collective-permute-start) | collective-permute-done | bytes 1638432 | tf_op jit(solution)/shard_map/ppermute | solution.py:46
  91.3 1.0 select_reduce_fusion
  92.2 0.1 broadcast_in_dim.51
  92.3 0.1 broadcast_xor_fusion
  92.4 0.2 select_reduce_fusion.1
  92.6 0.1 broadcast_subtract_fusion
  92.7 0.1 copy.32
  92.8 0.1 copy.31
  92.9 0.1 reshape_squeeze.9
  93.0 0.1 copy.36
  93.1 0.1 copy.35
  93.2 0.1 reshape_squeeze.10
  93.3 0.1 dynamic_slice.22
  93.4 0.1 dynamic_slice.24
  93.5 0.1 copy.40
  93.6 0.1 copy.39
  93.7 0.1 reshape_squeeze.11
  93.8 0.1 dynamic_slice.26
  93.9 2.0 collective-permute-start.8
  95.9 65.6 %collective-permute-done.3 = bf16[1280,640]{1,0:T(8,128)(2,1)} collective-permute-done((bf16[1280,640]{1,0:T(8,128)(2,1)}, bf16[1280,640]{1,0:T(8,128)(2,1)}, u32[]{:S(2)}, u32[]{:S(2)}) %collective-permute-start.3) | collective-permute-done | bytes 1638432 | tf_op jit(solution)/shard_map/ppermute | solution.py:46
  161.5 35.1 %collective-permute-done.6 = bf16[1280,640]{1,0:T(8,128)(2,1)} collective-permute-done((bf16[1280,640]{1,0:T(8,128)(2,1)}, bf16[1280,640]{1,0:T(8,128)(2,1)}, u32[]{:S(2)}, u32[]{:S(2)}) %collective-permute-start.6) | collective-permute-done | bytes 1638432 | tf_op jit(solution)/shard_map/ppermute | solution.py:46
  196.6 2.0 collective-permute-start.7
  198.6 68.2 %collective-permute-done.1 = bf16[1280,640]{1,0:T(8,128)(2,1)} collective-permute-done((bf16[1280,640]{1,0:T(8,128)(2,1)}, bf16[1280,640]{1,0:T(8,128)(2,1)}, u32[]{:S(2)}, u32[]{:S(2)}) %collective-permute-start.1) | collective-permute-done | bytes 1638432 | tf_op jit(solution)/shard_map/ppermute | solution.py:46
  266.8 57.5 %fusion.33 = f32[1280,640]{0,1:T(8,128)} fusion(bf16[1,160,8,5120]{3,2,0,1:T(8,128)(2,1)} %all-gather.7.cloned.1.call-done, s32[]{:T(128)S(6)} %select_n.37, bf16[1280,640]{1,0:T(8,128)(2,1)} %collective-permute-done.1, bf16[1280,640]{1,0:T(8,128)(2,1)} %collective-permute-done, bf16[1280,640]{1,0:T(8,128)(2,1)S(1)} %get-tuple-element.6, ...), kind=kOutput, calls=%fused_computation.54 | convolution fusion | flops 8441036800 | bytes 22937604 | tf_op jit(solution)/shard_map/dot_general | solution.py:55
  324.4 3.5 copy.30
  327.9 0.0 all-gather.9.cloned.1.call-done
  327.9 44.4 %fusion.38 = f32[1280,640]{0,1:T(8,128)} fusion(bf16[1,160,8,5120]{3,2,0,1:T(8,128)(2,1)} %all-gather.9.cloned.1.call-done, s32[]{:T(128)S(6)} %select_n.37, bf16[1280,640]{1,0:T(8,128)(2,1)} %collective-permute-done.4, bf16[1280,640]{1,0:T(8,128)(2,1)} %collective-permute-done.3, bf16[1280,640]{1,0:T(8,128)(2,1)} %get-tuple-element.8, ...), kind=kOutput, calls=%fused_computation.55 | convolution fusion | flops 8441036800 | bytes 22937604 | tf_op jit(solution)/shard_map/dot_general | solution.py:55
  372.3 4.6 %copy.34 = f32[1280,640]{1,0:T(8,128)} copy(f32[1280,640]{0,1:T(8,128)} %fusion.38) | data formatting | bytes 6553600 | tf_op jit(solution)/shard_map/dot_general | solution.py:55
  376.9 0.0 all-gather.11.cloned.1.call-done
  376.9 44.5 %fusion.43 = f32[1280,640]{0,1:T(8,128)} fusion(bf16[1,160,8,5120]{3,2,0,1:T(8,128)(2,1)} %all-gather.11.cloned.1.call-done, s32[]{:T(128)S(6)} %select_n.37, bf16[1280,640]{1,0:T(8,128)(2,1)} %collective-permute-done.7, bf16[1280,640]{1,0:T(8,128)(2,1)} %collective-permute-done.6, bf16[1280,640]{1,0:T(8,128)(2,1)} %get-tuple-element.7, ...), kind=kOutput, calls=%fused_computation.56 | convolution fusion | flops 8441036800 | bytes 22937604 | tf_op jit(solution)/shard_map/dot_general | solution.py:55
  421.4 4.6 %copy.38 = f32[1280,640]{1,0:T(8,128)} copy(f32[1280,640]{0,1:T(8,128)} %fusion.43) | data formatting | bytes 6553600 | tf_op jit(solution)/shard_map/dot_general | solution.py:55
  426.0 0.5 bitcast_divide_fusion.2
  426.5 1.4 copy-done
  427.9 0.5 bitcast_divide_fusion.1
  428.4 0.5 copy-done.1
  428.9 0.5 bitcast_divide_fusion
  429.4 4.5 %pad_maximum_fusion = f32[3,160,8,640]{3,2,1,0:T(8,128)} fusion(f32[1,160,8,640]{3,2,1,0:T(8,128)S(1)} %bitcast_divide_fusion, f32[1,160,8,640]{3,2,1,0:T(8,128)S(1)} %bitcast_divide_fusion.1, f32[1,160,8,640]{3,2,1,0:T(8,128)S(1)} %bitcast_divide_fusion.2), kind=kLoop, calls=%fused_computation.30 | loop fusion | flops 4915200 | bytes 19660800 | tf_op jit(solution)/shard_map/stack | solution.py:63
  (27 shorter events, 0.1 us)
Async XLA Ops:
  6.5 260.3 %all-gather.7.cloned.1.call-start = ((), (), s32[]{:S(2)}) async-start(), calls=%async_computation | async-start | bytes 14745600 | tf_op jit(solution)/shard_map/all_gather | solution.py:53
  11.3 316.5 %all-gather.9.cloned.1.call-start = ((), (), s32[]{:S(2)}) async-start(), calls=%async_computation.1 | async-start | bytes 14745600 | tf_op jit(solution)/shard_map/all_gather | solution.py:53
  11.4 79.9 %copy-start.2 = (f32[1280]{0:T(1024)S(1)}, f32[1280]{0:T(1024)}, u32[]{:S(2)}) copy-start(f32[1280]{0:T(1024)} %param.15) | copy-start | bytes 15364
  11.4 79.9 %copy-start.3 = (s32[1280]{0:T(1024)S(1)}, s32[1280]{0:T(1024)}, u32[]{:S(2)}) copy-start(s32[1280]{0:T(1024)} %param.12) | copy-start | bytes 15364
  11.4 80.9 %copy-start.5 = (s32[32]{0:T(128)S(1)}, s32[32]{0:T(128)}, u32[]{:S(2)}) copy-start(s32[32]{0:T(128)} %param.11) | copy-start | bytes 388
  11.4 80.9 %copy-start.6 = (s32[3]{0:T(128)S(1)}, s32[3]{0:T(128)}, u32[]{:S(2)}) copy-start(s32[3]{0:T(128)} %param.13) | copy-start | bytes 40
  11.4 81.2 %copy-start.4 = (f32[32]{0:T(128)S(1)}, f32[32]{0:T(128)}, u32[]{:S(2)}) copy-start(f32[32]{0:T(128)} %param.14) | copy-start | bytes 388
  12.1 364.8 %all-gather.11.cloned.1.call-start = ((), (), s32[]{:S(2)}) async-start(), calls=%async_computation.2 | async-start | bytes 14745600 | tf_op jit(solution)/shard_map/all_gather | solution.py:53
  17.4 73.9 %collective-permute-start = (bf16[1280,640]{1,0:T(8,128)(2,1)S(1)}, bf16[1280,640]{1,0:T(8,128)(2,1)}, u32[]{:S(2)}, u32[]{:S(2)}) collective-permute-start(bf16[1280,640]{1,0:T(8,128)(2,1)S(1)} %get-tuple-element.6), channel_id=1, source_target_pairs={{0,1},{1,2},{2,3},{3,0},{4,5},{5,6},{6,7},{7,4},{8,9},{9,10},{10,1... | collective-permute-start | bytes 4915208 | tf_op jit(solution)/shard_map/ppermute | solution.py:46
  17.4 76.5 %collective-permute-start.2 = (bf16[1280,640]{1,0:T(8,128)(2,1)S(1)}, bf16[1280,640]{1,0:T(8,128)(2,1)}, u32[]{:S(2)}, u32[]{:S(2)}) collective-permute-start(bf16[1280,640]{1,0:T(8,128)(2,1)S(1)} %get-tuple-element.6), channel_id=1, source_target_pairs={{0,3},{1,0},{2,1},{3,2},{4,7},{5,4},{6,5},{7,6},{8,11},{9,8},{10,9... | collective-permute-start | bytes 4915208 | tf_op jit(solution)/shard_map/ppermute | solution.py:48
  19.4 142.1 %collective-permute-start.3 = (bf16[1280,640]{1,0:T(8,128)(2,1)}, bf16[1280,640]{1,0:T(8,128)(2,1)}, u32[]{:S(2)}, u32[]{:S(2)}) collective-permute-start(bf16[1280,640]{1,0:T(8,128)(2,1)} %get-tuple-element.8), channel_id=1, source_target_pairs={{0,1},{1,2},{2,3},{3,0},{4,5},{5,6},{6,7},{7,4},{8,9},{9,10},{10,1... | collective-permute-start | bytes 4915208 | tf_op jit(solution)/shard_map/ppermute | solution.py:46
  21.2 306.6 %collective-permute-start.5 = (bf16[1280,640]{1,0:T(8,128)(2,1)}, bf16[1280,640]{1,0:T(8,128)(2,1)}, u32[]{:S(2)}, u32[]{:S(2)}) collective-permute-start(bf16[1280,640]{1,0:T(8,128)(2,1)} %get-tuple-element.8), channel_id=1, source_target_pairs={{0,3},{1,0},{2,1},{3,2},{4,7},{5,4},{6,5},{7,6},{8,11},{9,8},{10,9... | collective-permute-start | bytes 4915208 | tf_op jit(solution)/shard_map/ppermute | solution.py:48
  21.4 175.2 %collective-permute-start.6 = (bf16[1280,640]{1,0:T(8,128)(2,1)}, bf16[1280,640]{1,0:T(8,128)(2,1)}, u32[]{:S(2)}, u32[]{:S(2)}) collective-permute-start(bf16[1280,640]{1,0:T(8,128)(2,1)} %get-tuple-element.7), channel_id=1, source_target_pairs={{0,1},{1,2},{2,3},{3,0},{4,5},{5,6},{6,7},{7,4},{8,9},{9,10},{10,1... | collective-permute-start | bytes 4915208 | tf_op jit(solution)/shard_map/ppermute | solution.py:46
  91.3 175.6 %collective-permute-start.1 = (bf16[1280,640]{1,0:T(8,128)(2,1)}, bf16[1280,640]{1,0:T(8,128)(2,1)}, u32[]{:S(2)}, u32[]{:S(2)}) collective-permute-start(bf16[1280,640]{1,0:T(8,128)(2,1)} %collective-permute-done), channel_id=1, source_target_pairs={{0,1},{1,2},{2,3},{3,0},{4,5},{5,6},{6,7},{7,4},{8,9},{9,10},{10,1... | collective-permute-start | bytes 4915208 | tf_op jit(solution)/shard_map/ppermute | solution.py:46
  93.9 283.0 %collective-permute-start.8 = (bf16[1280,640]{1,0:T(8,128)(2,1)}, bf16[1280,640]{1,0:T(8,128)(2,1)}, u32[]{:S(2)}, u32[]{:S(2)}) collective-permute-start(bf16[1280,640]{1,0:T(8,128)(2,1)} %get-tuple-element.7), channel_id=1, source_target_pairs={{0,3},{1,0},{2,1},{3,2},{4,7},{5,4},{6,5},{7,6},{8,11},{9,8},{10,9... | collective-permute-start | bytes 4915208 | tf_op jit(solution)/shard_map/ppermute | solution.py:48
  161.5 166.4 %collective-permute-start.4 = (bf16[1280,640]{1,0:T(8,128)(2,1)}, bf16[1280,640]{1,0:T(8,128)(2,1)}, u32[]{:S(2)}, u32[]{:S(2)}) collective-permute-start(bf16[1280,640]{1,0:T(8,128)(2,1)} %collective-permute-done.3), channel_id=1, source_target_pairs={{0,1},{1,2},{2,3},{3,0},{4,5},{5,6},{6,7},{7,4},{8,9},{9,10},{10,1... | collective-permute-start | bytes 4915208 | tf_op jit(solution)/shard_map/ppermute | solution.py:46
  196.6 180.3 %collective-permute-start.7 = (bf16[1280,640]{1,0:T(8,128)(2,1)}, bf16[1280,640]{1,0:T(8,128)(2,1)}, u32[]{:S(2)}, u32[]{:S(2)}) collective-permute-start(bf16[1280,640]{1,0:T(8,128)(2,1)} %collective-permute-done.6), channel_id=1, source_target_pairs={{0,1},{1,2},{2,3},{3,0},{4,5},{5,6},{6,7},{7,4},{8,9},{9,10},{10,1... | collective-permute-start | bytes 4915208 | tf_op jit(solution)/shard_map/ppermute | solution.py:46
  426.0 1.9 copy-start
  426.0 2.9 copy-start.1
Sparse Core Ops, SparseCore 0:
  11.5 75.3 all-gather.6
  88.7 74.3 all-gather.8
  165.0 74.3 all-gather.10
